TPU v7x, 512 devices: a whole 4x4x16 slice. The times are simulated.
512 devices in a mesh: seq: 128 (over z, y, x_hi), branch: 4 (over x_lo, core).
Axes of the slice: x: 4 (x_hi: 2, x_lo: 2; x = x_hi * 2 + x_lo), y: 4, z: 16, core: 2. Of those that a mesh axis runs over, the one named last changes fastest.
Arguments:
- q_ctl: bfloat16 [4, 24576, 2048], P('branch', 'seq'), may hold values from -64 to 64
- k_ctl: bfloat16 [4, 24576, 2048], P('branch', 'seq'), may hold values from -64 to 64
- v_ctl: bfloat16 [4, 24576, 2048], P('branch', 'seq'), may hold values from -6 to 6
- positions: int32 [24576], P('seq'), may hold values from 0 to 12287
- branch_ids: int32 [4], P('branch'), may hold values from 0 to 63
- cond_scale: float32 [64], replicated, may hold values from 0.25 to 2
- out_weight: bfloat16 [2048, 3072], P('branch', 'seq'), may hold values from -0.125 to 0.125
- frozen: bfloat16 [24576, 3072], P(('seq', 'branch')), may hold values from -2.390625 to 2.390625
- norm_gain: float32 [3072], replicated, may hold values from 0.5 to 1.5
- cotangent: bfloat16 [24576, 3072], P('seq'), may hold values from -6 to 6
Outputs:
- normed: bfloat16 [24576, 3072], P(('seq', 'branch'))
- grad_attn: bfloat16 [4, 24576, 2048], P('branch', 'seq')
All inputs are finite; a program needn't handle non-finite values.
Results may differ from a plain program's by a relative error of at most 0.014.
Values may be sent and summed in bfloat16 or wider, within the bound.
No kernel may reach another device: no remote copies, remote signals or barrier semaphores. Data moves between devices by JAX's collectives and lax.ppermute only.
A program may use at most 64 MiB of HBM per device.

v0:
```python
import math
import jax
import jax.numpy as jnp
from jax import lax
from jax.sharding import PartitionSpec as P

HEADS = 16
HEAD_DIM = 128
EPS = 1e-06


def from_partner(shard, axis, distance):
    return lax.ppermute(shard, axis, [(i, i ^ 1 << distance) for i in range(lax.axis_size(axis))])


def rope_tables(positions, head_dim):
    exponents = jnp.arange(head_dim // 2, dtype=jnp.float32) * (2.0 / head_dim)
    frequencies = 10000.0 ** (-exponents)
    angles = positions.astype(jnp.float32)[..., None] * frequencies
    return (jnp.cos(angles), jnp.sin(angles))


def rotate(values_in, cosines, sines):
    half_dim = values_in.shape[-1] // 2
    front_half = values_in[..., :half_dim]
    back_half = values_in[..., half_dim:]
    return jnp.concatenate(
        [front_half * cosines - back_half * sines, back_half * cosines + front_half * sines],
        axis=-1,
    )


def normalize(hidden, norm_gain):
    inverse = lax.rsqrt(jnp.mean(hidden * hidden, axis=-1, keepdims=True) + EPS)
    return (hidden * inverse * norm_gain).astype(jnp.bfloat16)


def norm_grad(hidden, norm_gain, cotangent):
    inverse = lax.rsqrt(jnp.mean(hidden * hidden, axis=-1, keepdims=True) + EPS)
    upstream = cotangent.astype(jnp.float32) * norm_gain
    inner_mean = jnp.mean(upstream * hidden, axis=-1, keepdims=True)
    return (inverse * upstream - hidden * (inverse * inverse * inverse) * inner_mean).astype(
        jnp.bfloat16
    )


def attend_head(packed):
    query_rows, key_rows, value_rows = packed
    clip_len = query_rows.shape[0]
    block_rows = min(512, clip_len)
    factor = 1.0 / math.sqrt(query_rows.shape[-1])

    def one_block(query_block):
        scores = jnp.dot(query_block, key_rows.T, preferred_element_type=jnp.float32) * factor
        row_max = jnp.max(scores, axis=-1, keepdims=True)
        weights = jnp.exp(scores - row_max)
        row_total = jnp.sum(weights, axis=-1, keepdims=True)
        weights_low = (weights / row_total).astype(jnp.bfloat16)
        return jnp.dot(weights_low, value_rows, preferred_element_type=jnp.float32).astype(
            jnp.bfloat16
        )

    blocks = query_rows.reshape(clip_len // block_rows, block_rows, query_rows.shape[-1])
    return lax.map(one_block, blocks).reshape(clip_len, query_rows.shape[-1])


def regroup(buffer, group_bits, seq_index, forward):
    full_shape = buffer.shape
    split = buffer.reshape(full_shape[:1] + (2,) * group_bits + full_shape[2:])
    for bit in range(group_bits):
        axis_here = group_bits - bit
        mine = jnp.bitwise_and(jnp.right_shift(seq_index, bit), 1)
        other = 1 - mine
        outgoing = lax.dynamic_index_in_dim(split, other, axis_here, keepdims=True)
        if forward:
            incoming = from_partner(outgoing, "seq", bit)
        else:
            incoming = from_partner(outgoing, "seq", bit)
        split = lax.dynamic_update_index_in_dim(split, incoming, other, axis_here)
    return split.reshape(full_shape)


def on_device(
    q_ctl, k_ctl, v_ctl, positions, branch_ids, cond_scale, out_weight, frozen, norm_gain, cotangent
):
    branch_index = lax.axis_index("branch")
    quarters = lax.axis_size("branch")
    seq_index = lax.axis_index("seq")
    seq_devices = lax.axis_size("seq")
    group = min(HEADS, seq_devices)
    group_bits = group.bit_length() - 1
    local_len = q_ctl.shape[1]
    feature_width = q_ctl.shape[2]
    head_dim = HEAD_DIM
    head_count = feature_width // head_dim
    heads_here = head_count // group
    clip_len = group * local_len
    quarter_len = local_len // quarters
    model_width = cotangent.shape[1]
    cosines, sines = rope_tables(positions, head_dim)
    cosines = cosines[:, None, :]
    sines = sines[:, None, :]

    def heads_first(source, rotated):
        split_heads = source[0].reshape(local_len, head_count, head_dim)
        if rotated:
            split_heads = rotate(split_heads.astype(jnp.float32), cosines, sines).astype(
                jnp.bfloat16
            )
        split_heads = split_heads.reshape(local_len, group, heads_here, head_dim)
        return jnp.transpose(split_heads, (1, 0, 2, 3))

    stacked = jnp.stack(
        [heads_first(q_ctl, True), heads_first(k_ctl, True), heads_first(v_ctl, False)]
    )
    arrived = regroup(stacked, group_bits, seq_index, True)

    def per_head(member):
        return jnp.transpose(member, (2, 0, 1, 3)).reshape(heads_here, clip_len, head_dim)

    attended_heads = lax.map(
        attend_head, (per_head(arrived[0]), per_head(arrived[1]), per_head(arrived[2]))
    )
    going_back = jnp.transpose(
        attended_heads.reshape(heads_here, group, local_len, head_dim), (1, 2, 0, 3)
    )[None]
    returned = regroup(going_back, group_bits, seq_index, False)[0]
    attended = jnp.transpose(returned, (1, 0, 2, 3)).reshape(local_len, feature_width)
    branch_scale = jnp.sum(
        jnp.where(jnp.arange(cond_scale.shape[0]) == branch_ids[0], cond_scale, 0.0)
    )
    weight_rows = lax.all_gather(out_weight, "seq", axis=1, tiled=True)
    mixed = lax.psum_scatter(
        (branch_scale * attended.astype(jnp.float32)).astype(jnp.bfloat16),
        "branch",
        scatter_dimension=1,
        tiled=True,
    ).astype(jnp.float32)
    mixed_high = mixed.astype(jnp.bfloat16)
    mixed_rest = (mixed - mixed_high.astype(jnp.float32)).astype(jnp.bfloat16)
    partial_stream = jnp.dot(mixed_high, weight_rows, preferred_element_type=jnp.float32)
    partial_stream = partial_stream + jnp.dot(
        mixed_rest, weight_rows, preferred_element_type=jnp.float32
    )
    owner = (jnp.arange(quarters) == branch_index).astype(jnp.float32)[:, None, None]
    term = (
        partial_stream.reshape(quarters, quarter_len, model_width)
        + owner * frozen.astype(jnp.float32)[None]
    )
    hidden = (
        lax.psum(term.astype(jnp.bfloat16), "branch")
        .astype(jnp.float32)
        .reshape(local_len, model_width)
    )
    hidden_share = lax.dynamic_slice_in_dim(hidden, branch_index * quarter_len, quarter_len, 0)
    normed = normalize(hidden_share, norm_gain)
    grad_hidden = norm_grad(hidden, norm_gain, cotangent)
    cot_block = jnp.einsum(
        "td,hd->th", grad_hidden, weight_rows, preferred_element_type=jnp.float32
    ).astype(jnp.bfloat16)
    cot_attn = lax.all_gather(cot_block, "branch", axis=1, tiled=True)
    grad_attn = (branch_scale * cot_attn.astype(jnp.float32)).astype(jnp.bfloat16)
    return (normed, grad_attn.reshape(1, local_len, feature_width))


def solution(mesh):
    return jax.shard_map(
        on_device,
        mesh=mesh,
        in_specs=(
            P("branch", "seq", None),
            P("branch", "seq", None),
            P("branch", "seq", None),
            P("seq"),
            P("branch"),
            P(),
            P("branch", "seq"),
            P(("seq", "branch"), None),
            P(),
            P("seq", None),
        ),
        out_specs=(P(("seq", "branch"), None), P("branch", "seq", None)),
        check_vma=False,
    )
```

profile of v0, /device:TPU:1, one launch (start us, length us, event | category | flops | bytes accessed | tf_op | source)
XLA Modules:
  0.0 424.5 jit_solution(8821610244191821590)
XLA Ops:
  8.7 1.4 convert_bitcast_fusion.1
  15.9 1.6 pad_maximum_fusion
  18.6 5.4 %collective-permute-start = (bf16[3,2,2,2,1,192,1,128]{7,5,4,3,2,1,6,0:T(8,128)(2,1)}, bf16[3,2,2,2,1,192,1,128]{7,5,4,3,2,1,6,0:T(8,128)(2,1)S(1)}, u32[]{:S(2)}, u32[]{:S(2)}) collective-permute-start(bf16[3,2,2,2,1,192,1,128]{7,5,4,3,2,1,6,0:T(8,128)(2,1)} %constant_dynamic-slice_fusion.7), channel_id=1, source_target_pairs={{0,4},{4,0},{8,12},{12,8},{16,20},{20,16},{24,28},{28,24},{32,36},... | collective-permute-start | bytes 3538952 | tf_op jit(solution)/shard_map/ppermute | solution.py:13
  24.1 22.6 %collective-permute-done = bf16[3,2,2,2,1,192,1,128]{7,5,4,3,2,1,6,0:T(8,128)(2,1)S(1)} collective-permute-done((bf16[3,2,2,2,1,192,1,128]{7,5,4,3,2,1,6,0:T(8,128)(2,1)}, bf16[3,2,2,2,1,192,1,128]{7,5,4,3,2,1,6,0:T(8,128)(2,1)S(1)}, u32[]{:S(2)}, u32[]{:S(2)}) %collective-permute-start) | collective-permute-done | bytes 1179680 | tf_op jit(solution)/shard_map/ppermute | solution.py:13
  47.9 6.5 %collective-permute-start.1 = (bf16[3,2,2,1,2,192,1,128]{7,5,4,3,2,1,6,0:T(8,128)(2,1)}, bf16[3,2,2,1,2,192,1,128]{7,5,4,3,2,1,6,0:T(8,128)(2,1)S(1)}, u32[]{:S(2)}, u32[]{:S(2)}) collective-permute-start(bf16[3,2,2,1,2,192,1,128]{7,5,4,3,2,1,6,0:T(8,128)(2,1)} %constant_dynamic-slice_fusion.6), channel_id=1, source_target_pairs={{0,8},{4,12},{8,0},{12,4},{16,24},{20,28},{24,16},{28,20},{32,40},... | collective-permute-start | bytes 3538952 | tf_op jit(solution)/shard_map/ppermute | solution.py:13
  54.4 24.8 %collective-permute-done.1 = bf16[3,2,2,1,2,192,1,128]{7,5,4,3,2,1,6,0:T(8,128)(2,1)S(1)} collective-permute-done((bf16[3,2,2,1,2,192,1,128]{7,5,4,3,2,1,6,0:T(8,128)(2,1)}, bf16[3,2,2,1,2,192,1,128]{7,5,4,3,2,1,6,0:T(8,128)(2,1)S(1)}, u32[]{:S(2)}, u32[]{:S(2)}) %collective-permute-start.1) | collective-permute-done | bytes 1179680 | tf_op jit(solution)/shard_map/ppermute | solution.py:13
  80.5 4.9 %collective-permute-start.2 = (bf16[3,2,1,2,2,192,1,128]{7,5,4,3,2,1,6,0:T(8,128)(2,1)}, bf16[3,2,1,2,2,192,1,128]{7,5,4,3,2,1,6,0:T(8,128)(2,1)S(1)}, u32[]{:S(2)}, u32[]{:S(2)}) collective-permute-start(bf16[3,2,1,2,2,192,1,128]{7,5,4,3,2,1,6,0:T(8,128)(2,1)} %constant_dynamic-slice_fusion.5), channel_id=1, source_target_pairs={{0,16},{4,20},{8,24},{12,28},{16,0},{20,4},{24,8},{28,12},{32,48},... | collective-permute-start | bytes 3538952 | tf_op jit(solution)/shard_map/ppermute | solution.py:13
  85.4 24.0 %collective-permute-done.2 = bf16[3,2,1,2,2,192,1,128]{7,5,4,3,2,1,6,0:T(8,128)(2,1)S(1)} collective-permute-done((bf16[3,2,1,2,2,192,1,128]{7,5,4,3,2,1,6,0:T(8,128)(2,1)}, bf16[3,2,1,2,2,192,1,128]{7,5,4,3,2,1,6,0:T(8,128)(2,1)S(1)}, u32[]{:S(2)}, u32[]{:S(2)}) %collective-permute-start.2) | collective-permute-done | bytes 1179680 | tf_op jit(solution)/shard_map/ppermute | solution.py:13
  110.8 3.5 collective-permute-start.3
  114.3 23.2 %collective-permute-done.3 = bf16[3,1,2,2,2,192,1,128]{7,5,4,3,2,1,6,0:T(8,128)(2,1)S(1)} collective-permute-done((bf16[3,1,2,2,2,192,1,128]{7,5,4,3,2,1,6,0:T(8,128)(2,1)}, bf16[3,1,2,2,2,192,1,128]{7,5,4,3,2,1,6,0:T(8,128)(2,1)S(1)}, u32[]{:S(2)}, u32[]{:S(2)}) %collective-permute-start.3) | collective-permute-done | bytes 1179680 | tf_op jit(solution)/shard_map/ppermute | solution.py:13
  137.7 1.4 fusion.22
  139.0 31.2 %while.17 = (s32[]{:T(128)}, bf16[6,512,128]{2,1,0:T(8,128)(2,1)}, bf16[6,512,128]{2,1,0:T(8,128)(2,1)}, bf16[3072,128]{1,0:T(8,128)(2,1)S(1)}, bf16[3072,128]{1,0:T(8,128)(2,1)}, /*index=5*/s32[]{:T(128)}) while((s32[]{:T(128)}, bf16[6,512,128]{2,1,0:T(8,128)(2,1)}, bf16[6,512,128]{2,1,0:T(8,128)(2,1)}, bf16[3072,128]{1,0:T(8,128)(2,1)S(1)}, ...), condition=%wide.region_4.5_spmd, body=%wide.region_1.4_spmd.sunk | while | flops 819526656 | bytes 23866464 | solution.py:64
  139.0 2.0 multiply_reduce_fusion.5
  141.0 1.2 fusion.36
  142.2 2.1 fusion.37
  144.2 2.0 multiply_reduce_fusion.5
  146.2 1.2 fusion.36
  147.4 2.1 fusion.37
  149.4 2.0 multiply_reduce_fusion.5
  151.4 1.2 fusion.36
  152.6 2.1 fusion.37
  154.6 2.0 multiply_reduce_fusion.5
  156.6 1.2 fusion.36
  157.8 2.1 fusion.37
  159.8 2.0 multiply_reduce_fusion.5
  161.8 1.2 fusion.36
  163.0 2.1 fusion.37
  165.0 2.0 multiply_reduce_fusion.5
  167.0 1.2 fusion.36
  168.2 2.1 fusion.37
  171.3 4.6 %collective-permute-start.4 = (bf16[1,2,2,2,1,192,1,128]{7,5,4,3,2,1,6,0:T(8,128)(2,1)S(1)}, bf16[1,2,2,2,1,192,1,128]{7,5,4,3,2,1,6,0:T(8,128)(2,1)S(1)}, u32[]{:S(2)}, u32[]{:S(2)}) collective-permute-start(bf16[1,2,2,2,1,192,1,128]{7,5,4,3,2,1,6,0:T(8,128)(2,1)S(1)} %constant_dynamic-slice_fusion.3), channel_id=1, source_target_pairs={{0,4},{4,0},{8,12},{12,8},{16,20},{20,16},{24,28},{28,24},{32,36},... | collective-permute-start | bytes 1179656 | tf_op jit(solution)/shard_map/ppermute | solution.py:13
  175.9 5.4 %collective-permute-done.4 = bf16[1,2,2,2,1,192,1,128]{7,5,4,3,2,1,6,0:T(8,128)(2,1)S(1)} collective-permute-done((bf16[1,2,2,2,1,192,1,128]{7,5,4,3,2,1,6,0:T(8,128)(2,1)S(1)}, bf16[1,2,2,2,1,192,1,128]{7,5,4,3,2,1,6,0:T(8,128)(2,1)S(1)}, u32[]{:S(2)}, u32[]{:S(2)}) %collective-permute-start.4) | collective-permute-done | bytes 393248 | tf_op jit(solution)/shard_map/ppermute | solution.py:13
  183.2 3.2 collective-permute-start.5
  186.3 5.7 %collective-permute-done.5 = bf16[1,2,2,1,2,192,1,128]{7,5,4,3,2,1,6,0:T(8,128)(2,1)S(1)} collective-permute-done((bf16[1,2,2,1,2,192,1,128]{7,5,4,3,2,1,6,0:T(8,128)(2,1)S(1)}, bf16[1,2,2,1,2,192,1,128]{7,5,4,3,2,1,6,0:T(8,128)(2,1)S(1)}, u32[]{:S(2)}, u32[]{:S(2)}) %collective-permute-start.5) | collective-permute-done | bytes 393248 | tf_op jit(solution)/shard_map/ppermute | solution.py:13
  193.9 4.8 %collective-permute-start.6 = (bf16[1,2,1,2,2,192,1,128]{7,5,4,3,2,1,6,0:T(8,128)(2,1)S(1)}, bf16[1,2,1,2,2,192,1,128]{7,5,4,3,2,1,6,0:T(8,128)(2,1)S(1)}, u32[]{:S(2)}, u32[]{:S(2)}) collective-permute-start(bf16[1,2,1,2,2,192,1,128]{7,5,4,3,2,1,6,0:T(8,128)(2,1)S(1)} %constant_dynamic-slice_fusion.1), channel_id=1, source_target_pairs={{0,16},{4,20},{8,24},{12,28},{16,0},{20,4},{24,8},{28,12},{32,48},... | collective-permute-start | bytes 1179656 | tf_op jit(solution)/shard_map/ppermute | solution.py:13
  198.7 5.2 %collective-permute-done.6 = bf16[1,2,1,2,2,192,1,128]{7,5,4,3,2,1,6,0:T(8,128)(2,1)S(1)} collective-permute-done((bf16[1,2,1,2,2,192,1,128]{7,5,4,3,2,1,6,0:T(8,128)(2,1)S(1)}, bf16[1,2,1,2,2,192,1,128]{7,5,4,3,2,1,6,0:T(8,128)(2,1)S(1)}, u32[]{:S(2)}, u32[]{:S(2)}) %collective-permute-start.6) | collective-permute-done | bytes 393248 | tf_op jit(solution)/shard_map/ppermute | solution.py:13
  205.8 3.5 collective-permute-start.7
  210.6 4.3 %collective-permute-done.7 = bf16[1,1,2,2,2,192,1,128]{7,5,4,3,2,1,6,0:T(8,128)(2,1)S(1)} collective-permute-done((bf16[1,1,2,2,2,192,1,128]{7,5,4,3,2,1,6,0:T(8,128)(2,1)S(1)}, bf16[1,1,2,2,2,192,1,128]{7,5,4,3,2,1,6,0:T(8,128)(2,1)S(1)}, u32[]{:S(2)}, u32[]{:S(2)}) %collective-permute-start.7) | collective-permute-done | bytes 393248 | tf_op jit(solution)/shard_map/ppermute | solution.py:13
  215.6 2.0 multiply_convert_fusion.1
  220.4 109.9 %all-gather.2.cloned.1.call-done = bf16[512,3072]{0,1:T(8,128)(2,1)} async-done(((bf16[512,24]{0,1:T(8,128)(2,1)}), bf16[512,3072]{0,1:T(8,128)(2,1)}) %all-gather.2.cloned.1.call-update) | async-done | bytes 3145744 | tf_op jit(solution)/shard_map/all_gather | solution.py:132
  330.4 3.3 fusion.23
  333.7 1.2 convolution_add_fusion
  334.9 1.3 add_convert_fusion
  336.3 62.4 %all-reduce.2.cloned.1.call-done = bf16[4,48,3072]{2,1,0:T(8,128)(2,1)} async-done(((bf16[4,48,3072]{2,1,0:T(8,128)(2,1)}), bf16[4,48,3072]{2,1,0:T(8,128)(2,1)}) %all-reduce.2.cloned.1.call-update) | async-done | bytes 1179664 | tf_op jit(solution)/shard_map/psum | solution.py:151
  398.7 3.5 multiply_reduce_fusion.1
  402.7 2.8 fusion.15
  405.5 8.8 %all_gather.7 = bf16[192,2048]{1,0:T(8,128)(2,1)S(1)} all-gather(bf16[192,512]{1,0:T(8,128)(2,1)S(1)} %fusion.15), channel_id=1, replica_groups=mesh['seq'=128,'branch'=4] {'branch'}, dimensions={1}, use_global_device_ids=true | all-gather | bytes 983040 | tf_op jit(solution)/shard_map/all_gather | solution.py:161
  414.4 1.7 fusion.20
  (81 shorter events, 24.0 us)
Async XLA Ops:
  8.0 322.4 %all-gather.2.cloned.1.call-start = ((), (), s32[]{:S(2)}) async-start(), calls=%async_computation.2 | async-start | bytes 3170304 | tf_op jit(solution)/shard_map/all_gather | solution.py:132
  8.7 1.7 copy-start.7
  13.3 1.3 copy-start.6
  18.6 28.0 %collective-permute-start = (bf16[3,2,2,2,1,192,1,128]{7,5,4,3,2,1,6,0:T(8,128)(2,1)}, bf16[3,2,2,2,1,192,1,128]{7,5,4,3,2,1,6,0:T(8,128)(2,1)S(1)}, u32[]{:S(2)}, u32[]{:S(2)}) collective-permute-start(bf16[3,2,2,2,1,192,1,128]{7,5,4,3,2,1,6,0:T(8,128)(2,1)} %constant_dynamic-slice_fusion.7), channel_id=1, source_target_pairs={{0,4},{4,0},{8,12},{12,8},{16,20},{20,16},{24,28},{28,24},{32,36},... | collective-permute-start | bytes 3538952 | tf_op jit(solution)/shard_map/ppermute | solution.py:13
  47.9 31.3 %collective-permute-start.1 = (bf16[3,2,2,1,2,192,1,128]{7,5,4,3,2,1,6,0:T(8,128)(2,1)}, bf16[3,2,2,1,2,192,1,128]{7,5,4,3,2,1,6,0:T(8,128)(2,1)S(1)}, u32[]{:S(2)}, u32[]{:S(2)}) collective-permute-start(bf16[3,2,2,1,2,192,1,128]{7,5,4,3,2,1,6,0:T(8,128)(2,1)} %constant_dynamic-slice_fusion.6), channel_id=1, source_target_pairs={{0,8},{4,12},{8,0},{12,4},{16,24},{20,28},{24,16},{28,20},{32,40},... | collective-permute-start | bytes 3538952 | tf_op jit(solution)/shard_map/ppermute | solution.py:13
  80.5 28.9 %collective-permute-start.2 = (bf16[3,2,1,2,2,192,1,128]{7,5,4,3,2,1,6,0:T(8,128)(2,1)}, bf16[3,2,1,2,2,192,1,128]{7,5,4,3,2,1,6,0:T(8,128)(2,1)S(1)}, u32[]{:S(2)}, u32[]{:S(2)}) collective-permute-start(bf16[3,2,1,2,2,192,1,128]{7,5,4,3,2,1,6,0:T(8,128)(2,1)} %constant_dynamic-slice_fusion.5), channel_id=1, source_target_pairs={{0,16},{4,20},{8,24},{12,28},{16,0},{20,4},{24,8},{28,12},{32,48},... | collective-permute-start | bytes 3538952 | tf_op jit(solution)/shard_map/ppermute | solution.py:13
  110.8 26.7 %collective-permute-start.3 = (bf16[3,1,2,2,2,192,1,128]{7,5,4,3,2,1,6,0:T(8,128)(2,1)}, bf16[3,1,2,2,2,192,1,128]{7,5,4,3,2,1,6,0:T(8,128)(2,1)S(1)}, u32[]{:S(2)}, u32[]{:S(2)}) collective-permute-start(bf16[3,1,2,2,2,192,1,128]{7,5,4,3,2,1,6,0:T(8,128)(2,1)} %constant_dynamic-slice_fusion.4), channel_id=1, source_target_pairs={{0,32},{4,36},{8,40},{12,44},{16,48},{20,52},{24,56},{28,60},{32,0... | collective-permute-start | bytes 3538952 | tf_op jit(solution)/shard_map/ppermute | solution.py:13
  114.3 216.1 %reduce-scatter.2.cloned.1.call-start = ((), (), s32[]{:S(2)}) async-start(), calls=%async_computation.1 | async-start | bytes 983040 | tf_op jit(solution)/shard_map/reduce_scatter | solution.py:133
  141.0 1.2 copy-start.4
  146.2 1.2 copy-start.4
  151.4 1.2 copy-start.4
  156.6 1.2 copy-start.4
  161.8 1.2 copy-start.4
  167.0 1.2 copy-start.4
  171.3 38.6 %copy-start.10 = (f32[64]{0:T(128)S(1)}, f32[64]{0:T(128)}, u32[]{:S(2)}) copy-start(f32[64]{0:T(128)} %param.17) | copy-start | bytes 772
  171.3 10.0 %collective-permute-start.4 = (bf16[1,2,2,2,1,192,1,128]{7,5,4,3,2,1,6,0:T(8,128)(2,1)S(1)}, bf16[1,2,2,2,1,192,1,128]{7,5,4,3,2,1,6,0:T(8,128)(2,1)S(1)}, u32[]{:S(2)}, u32[]{:S(2)}) collective-permute-start(bf16[1,2,2,2,1,192,1,128]{7,5,4,3,2,1,6,0:T(8,128)(2,1)S(1)} %constant_dynamic-slice_fusion.3), channel_id=1, source_target_pairs={{0,4},{4,0},{8,12},{12,8},{16,20},{20,16},{24,28},{28,24},{32,36},... | collective-permute-start | bytes 1179656 | tf_op jit(solution)/shard_map/ppermute | solution.py:13
  183.2 8.9 %collective-permute-start.5 = (bf16[1,2,2,1,2,192,1,128]{7,5,4,3,2,1,6,0:T(8,128)(2,1)S(1)}, bf16[1,2,2,1,2,192,1,128]{7,5,4,3,2,1,6,0:T(8,128)(2,1)S(1)}, u32[]{:S(2)}, u32[]{:S(2)}) collective-permute-start(bf16[1,2,2,1,2,192,1,128]{7,5,4,3,2,1,6,0:T(8,128)(2,1)S(1)} %constant_dynamic-slice_fusion.2), channel_id=1, source_target_pairs={{0,8},{4,12},{8,0},{12,4},{16,24},{20,28},{24,16},{28,20},{32,40},... | collective-permute-start | bytes 1179656 | tf_op jit(solution)/shard_map/ppermute | solution.py:13
  193.9 10.0 %collective-permute-start.6 = (bf16[1,2,1,2,2,192,1,128]{7,5,4,3,2,1,6,0:T(8,128)(2,1)S(1)}, bf16[1,2,1,2,2,192,1,128]{7,5,4,3,2,1,6,0:T(8,128)(2,1)S(1)}, u32[]{:S(2)}, u32[]{:S(2)}) collective-permute-start(bf16[1,2,1,2,2,192,1,128]{7,5,4,3,2,1,6,0:T(8,128)(2,1)S(1)} %constant_dynamic-slice_fusion.1), channel_id=1, source_target_pairs={{0,16},{4,20},{8,24},{12,28},{16,0},{20,4},{24,8},{28,12},{32,48},... | collective-permute-start | bytes 1179656 | tf_op jit(solution)/shard_map/ppermute | solution.py:13
  205.8 9.1 %collective-permute-start.7 = (bf16[1,1,2,2,2,192,1,128]{7,5,4,3,2,1,6,0:T(8,128)(2,1)S(1)}, bf16[1,1,2,2,2,192,1,128]{7,5,4,3,2,1,6,0:T(8,128)(2,1)S(1)}, u32[]{:S(2)}, u32[]{:S(2)}) collective-permute-start(bf16[1,1,2,2,2,192,1,128]{7,5,4,3,2,1,6,0:T(8,128)(2,1)S(1)} %constant_dynamic-slice_fusion), channel_id=1, source_target_pairs={{0,32},{4,36},{8,40},{12,44},{16,48},{20,52},{24,56},{28,60},{32,0... | collective-permute-start | bytes 1179656 | tf_op jit(solution)/shard_map/ppermute | solution.py:13
  217.6 2.0 copy-start.8
  219.5 179.2 %all-reduce.2.cloned.1.call-start = ((), (), s32[]{:S(2)}) async-start(), calls=%async_computation.3 | async-start | bytes 2359296 | tf_op jit(solution)/shard_map/psum | solution.py:151
  330.4 3.3 copy-start
  330.4 3.3 copy-start.5
  333.7 1.2 copy-start.3
  334.9 63.8 %copy-start.9 = (f32[3072]{0:T(1024)S(1)}, f32[3072]{0:T(1024)}, u32[]{:S(2)}) copy-start(f32[3072]{0:T(1024)} %param.20) | copy-start | bytes 36868
  398.7 3.5 copy-start.2
  405.5 10.5 %copy-start.1 = (f32[192,3072]{1,0:T(8,128)S(1)}, f32[192,3072]{1,0:T(8,128)}, u32[]{:S(2)}) copy-start(f32[192,3072]{1,0:T(8,128)} %get-tuple-element.56) | copy-start | bytes 7077892
Sparse Core Ops, SparseCore 0:
  114.4 215.9 all-gather.1
Sparse Core Ops, SparseCore 1:
  219.6 39.7 reduce-scatter.1
  336.4 62.3 all-reduce.1
where the time goes:
time: 425 us; the launch traced here: 424 us
  waiting for transfers between devices  288 us (68%)
  starting transfers between devices  36.4 us (9%)
  matrix products  31.5 us (7%)
  other arithmetic  24.5 us (6%)
  local copies, waits for them, and re-layouts  19.1 us (4%)
  between operations  16.5 us (4%)
  blocking collectives  8.84 us (2%)
    ppermute x8, waiting for transfers between devices, from_partner(): lax.ppermute(shard, axis, [(i, i ^ 1 << distance) for i in range(lax.axis...  115 us
    all_gather x1, waiting for transfers between devices, on_device(): weight_rows = lax.all_gather(out_weight, 'seq', axis=1, tiled=True)  110 us
    psum x1, waiting for transfers between devices, on_device(): lax.psum(term.astype(jnp.bfloat16), 'branch').astype(jnp.float32)  62.4 us
    ppermute x8, starting transfers between devices, from_partner(): lax.ppermute(shard, axis, [(i, i ^ 1 << distance) for i in range(lax.axis...  36.3 us
    dot_general x6, matrix products, one_block(): jnp.dot(weights_low, value_rows, preferred_element_type=jnp.float32)  12.4 us
    dot_general x6, matrix products, one_block(): jnp.dot(query_block, key_rows.T, preferred_element_type=jnp.float32)  11.8 us
    all_gather x1, blocking collectives, on_device(): cot_attn = lax.all_gather(cot_block, 'branch', axis=1, tiled=True)  8.84 us
    dynamic_slice x8, local copies, waits for them, and re-layouts, regroup(): outgoing = lax.dynamic_index_in_dim(split, other, axis_here, keepdims=True)  8.65 us
  transfers between devices with their start and end apart: 11, of which 10 were waited for; matrix products, arithmetic and copies ran while one was open for 11% of the time, Pallas kernels for 0%

commit v1 on v0

--- a/solution.py
+++ b/solution.py
@@ -129,7 +129,9 @@
     branch_scale = jnp.sum(
         jnp.where(jnp.arange(cond_scale.shape[0]) == branch_ids[0], cond_scale, 0.0)
     )
-    weight_rows = lax.all_gather(out_weight, "seq", axis=1, tiled=True)
+    weight_rows = jnp.concatenate(
+        lax.all_to_all(jnp.stack([out_weight] * lax.axis_size("seq")), "seq", 0, 0), axis=1
+    )
     mixed = lax.psum_scatter(
         (branch_scale * attended.astype(jnp.float32)).astype(jnp.bfloat16),
         "branch",

time: 425 us -> 413 us (0.972)
  waiting for transfers between devices: 288 us -> 256 us
  starting transfers between devices: 36.4 us -> 53.8 us
    all_gather x1 -> x0, waiting for transfers between devices: 110 us -> none  [on_device(): weight_rows = lax.all_gather(out_weight, 'seq', axis=1, tiled=True)]
    ppermute x8, waiting for transfers between devices: 115 us -> 162 us  [from_partner(): lax.ppermute(shard, axis, [(i, i ^ 1 << distance) for i in range(lax.axis...]
    reduce_scatter x1, waiting for transfers between devices: 0.01 us -> 34.9 us  [on_device(): lax.psum_scatter((branch_scale * attended.astype(jnp.float32)).astype(jnp...]
    all_to_all x0 -> x1, starting transfers between devices: none -> 21.7 us  [on_device(): lax.all_to_all(jnp.stack([out_weight] * lax.axis_size('seq')), 'seq', 0, 0)]
    ppermute x8, starting transfers between devices: 36.3 us -> 31.9 us  [from_partner(): lax.ppermute(shard, axis, [(i, i ^ 1 << distance) for i in range(lax.axis...]
  transfers between devices with their start and end apart: 11 -> 11, of which waited for: 10 -> 9; matrix products, arithmetic and copies ran while one was open for 11% -> 11% of each run, Pallas kernels for 0% -> 0%
where the time goes in v1:
time: 413 us; the launch traced here: 411 us
  waiting for transfers between devices  256 us (62%)
  starting transfers between devices  53.8 us (13%)
  matrix products  33.3 us (8%)
  other arithmetic  23.1 us (6%)
  local copies, waits for them, and re-layouts  21.6 us (5%)
  between operations  15.1 us (4%)
  blocking collectives  8.71 us (2%)
    ppermute x8, waiting for transfers between devices, from_partner(): lax.ppermute(shard, axis, [(i, i ^ 1 << distance) for i in range(lax.axis...  162 us
    psum x1, waiting for transfers between devices, on_device(): lax.psum(term.astype(jnp.bfloat16), 'branch').astype(jnp.float32)  59.1 us
    reduce_scatter x1, waiting for transfers between devices, on_device(): lax.psum_scatter((branch_scale * attended.astype(jnp.float32)).astype(jnp...  34.9 us
    ppermute x8, starting transfers between devices, from_partner(): lax.ppermute(shard, axis, [(i, i ^ 1 << distance) for i in range(lax.axis...  31.9 us
    all_to_all x1, starting transfers between devices, on_device(): lax.all_to_all(jnp.stack([out_weight] * lax.axis_size('seq')), 'seq', 0, 0)  21.7 us
    dot_general x6, matrix products, one_block(): jnp.dot(weights_low, value_rows, preferred_element_type=jnp.float32)  12.4 us
    dot_general x6, matrix products, one_block(): jnp.dot(query_block, key_rows.T, preferred_element_type=jnp.float32)  11.8 us
    all_gather x1, blocking collectives, on_device(): cot_attn = lax.all_gather(cot_block, 'branch', axis=1, tiled=True)  8.71 us
  transfers between devices with their start and end apart: 11, of which 9 were waited for; matrix products, arithmetic and copies ran while one was open for 11% of the time, Pallas kernels for 0%

profile of v1, /device:TPU:1, one launch (start us, length us, event | category | flops | bytes accessed | tf_op | source)
XLA Modules:
  0.0 411.5 jit_solution(10611426497792304768)
XLA Ops:
  7.9 1.4 convert_bitcast_fusion.1
  15.0 1.6 pad_maximum_fusion
  17.7 5.4 %collective-permute-start = (bf16[3,2,2,2,1,192,1,128]{7,5,4,3,2,1,6,0:T(8,128)(2,1)}, bf16[3,2,2,2,1,192,1,128]{7,5,4,3,2,1,6,0:T(8,128)(2,1)S(1)}, u32[]{:S(2)}, u32[]{:S(2)}) collective-permute-start(bf16[3,2,2,2,1,192,1,128]{7,5,4,3,2,1,6,0:T(8,128)(2,1)} %constant_dynamic-slice_fusion.7), channel_id=1, source_target_pairs={{0,4},{4,0},{8,12},{12,8},{16,20},{20,16},{24,28},{28,24},{32,36},... | collective-permute-start | bytes 3538952 | tf_op jit(solution)/shard_map/ppermute | solution.py:13
  23.2 22.6 %collective-permute-done = bf16[3,2,2,2,1,192,1,128]{7,5,4,3,2,1,6,0:T(8,128)(2,1)S(1)} collective-permute-done((bf16[3,2,2,2,1,192,1,128]{7,5,4,3,2,1,6,0:T(8,128)(2,1)}, bf16[3,2,2,2,1,192,1,128]{7,5,4,3,2,1,6,0:T(8,128)(2,1)S(1)}, u32[]{:S(2)}, u32[]{:S(2)}) %collective-permute-start) | collective-permute-done | bytes 1179680 | tf_op jit(solution)/shard_map/ppermute | solution.py:13
  47.1 6.5 %collective-permute-start.1 = (bf16[3,2,2,1,2,192,1,128]{7,5,4,3,2,1,6,0:T(8,128)(2,1)}, bf16[3,2,2,1,2,192,1,128]{7,5,4,3,2,1,6,0:T(8,128)(2,1)S(1)}, u32[]{:S(2)}, u32[]{:S(2)}) collective-permute-start(bf16[3,2,2,1,2,192,1,128]{7,5,4,3,2,1,6,0:T(8,128)(2,1)} %constant_dynamic-slice_fusion.6), channel_id=1, source_target_pairs={{0,8},{4,12},{8,0},{12,4},{16,24},{20,28},{24,16},{28,20},{32,40},... | collective-permute-start | bytes 3538952 | tf_op jit(solution)/shard_map/ppermute | solution.py:13
  53.5 24.8 %collective-permute-done.1 = bf16[3,2,2,1,2,192,1,128]{7,5,4,3,2,1,6,0:T(8,128)(2,1)S(1)} collective-permute-done((bf16[3,2,2,1,2,192,1,128]{7,5,4,3,2,1,6,0:T(8,128)(2,1)}, bf16[3,2,2,1,2,192,1,128]{7,5,4,3,2,1,6,0:T(8,128)(2,1)S(1)}, u32[]{:S(2)}, u32[]{:S(2)}) %collective-permute-start.1) | collective-permute-done | bytes 1179680 | tf_op jit(solution)/shard_map/ppermute | solution.py:13
  79.7 4.9 %collective-permute-start.2 = (bf16[3,2,1,2,2,192,1,128]{7,5,4,3,2,1,6,0:T(8,128)(2,1)}, bf16[3,2,1,2,2,192,1,128]{7,5,4,3,2,1,6,0:T(8,128)(2,1)S(1)}, u32[]{:S(2)}, u32[]{:S(2)}) collective-permute-start(bf16[3,2,1,2,2,192,1,128]{7,5,4,3,2,1,6,0:T(8,128)(2,1)} %constant_dynamic-slice_fusion.5), channel_id=1, source_target_pairs={{0,16},{4,20},{8,24},{12,28},{16,0},{20,4},{24,8},{28,12},{32,48},... | collective-permute-start | bytes 3538952 | tf_op jit(solution)/shard_map/ppermute | solution.py:13
  84.6 24.0 %collective-permute-done.2 = bf16[3,2,1,2,2,192,1,128]{7,5,4,3,2,1,6,0:T(8,128)(2,1)S(1)} collective-permute-done((bf16[3,2,1,2,2,192,1,128]{7,5,4,3,2,1,6,0:T(8,128)(2,1)}, bf16[3,2,1,2,2,192,1,128]{7,5,4,3,2,1,6,0:T(8,128)(2,1)S(1)}, u32[]{:S(2)}, u32[]{:S(2)}) %collective-permute-start.2) | collective-permute-done | bytes 1179680 | tf_op jit(solution)/shard_map/ppermute | solution.py:13
  109.9 3.5 collective-permute-start.3
  113.4 1.9 stack.14
  115.3 21.7 %all-to-all-start = ((bf16[128,512,24]{1,2,0:T(8,128)(2,1)}), bf16[128,512,24]{1,2,0:T(8,128)(2,1)}, u32[]{:S(2)}, u32[]{:S(2)}) async-start(bf16[128,512,24]{1,2,0:T(8,128)(2,1)} %stack.14), calls=%async_computation.1 | async-start | bytes 6291456 | tf_op jit(solution)/shard_map/all_to_all | solution.py:133
  137.4 1.4 fusion.22
  138.7 31.2 %while.17 = (s32[]{:T(128)}, bf16[6,512,128]{2,1,0:T(8,128)(2,1)}, bf16[6,512,128]{2,1,0:T(8,128)(2,1)}, bf16[3072,128]{1,0:T(8,128)(2,1)S(1)}, bf16[3072,128]{1,0:T(8,128)(2,1)}, /*index=5*/s32[]{:T(128)}) while((s32[]{:T(128)}, bf16[6,512,128]{2,1,0:T(8,128)(2,1)}, bf16[6,512,128]{2,1,0:T(8,128)(2,1)}, bf16[3072,128]{1,0:T(8,128)(2,1)S(1)}, ...), condition=%wide.region_4.5_spmd, body=%wide.region_1.4_spmd.sunk | while | flops 819526656 | bytes 23866464 | solution.py:64
  138.7 2.0 multiply_reduce_fusion.5
  140.7 1.2 fusion.36
  141.9 2.1 fusion.37
  144.0 2.0 multiply_reduce_fusion.5
  145.9 1.2 fusion.36
  147.1 2.1 fusion.37
  149.2 2.0 multiply_reduce_fusion.5
  151.1 1.2 fusion.36
  152.3 2.1 fusion.37
  154.4 2.0 multiply_reduce_fusion.5
  156.3 1.2 fusion.36
  157.5 2.1 fusion.37
  159.6 2.0 multiply_reduce_fusion.5
  161.5 1.2 fusion.36
  162.7 2.1 fusion.37
  164.8 2.0 multiply_reduce_fusion.5
  167.9 2.1 fusion.37
  171.0 4.0 collective-permute-start.4
  175.1 7.7 %collective-permute-done.4 = bf16[1,2,2,2,1,192,1,128]{7,5,4,3,2,1,6,0:T(8,128)(2,1)S(1)} collective-permute-done((bf16[1,2,2,2,1,192,1,128]{7,5,4,3,2,1,6,0:T(8,128)(2,1)S(1)}, bf16[1,2,2,2,1,192,1,128]{7,5,4,3,2,1,6,0:T(8,128)(2,1)S(1)}, u32[]{:S(2)}, u32[]{:S(2)}) %collective-permute-start.4) | collective-permute-done | bytes 393248 | tf_op jit(solution)/shard_map/ppermute | solution.py:13
  184.6 2.8 collective-permute-start.5
  187.4 7.6 %collective-permute-done.5 = bf16[1,2,2,1,2,192,1,128]{7,5,4,3,2,1,6,0:T(8,128)(2,1)S(1)} collective-permute-done((bf16[1,2,2,1,2,192,1,128]{7,5,4,3,2,1,6,0:T(8,128)(2,1)S(1)}, bf16[1,2,2,1,2,192,1,128]{7,5,4,3,2,1,6,0:T(8,128)(2,1)S(1)}, u32[]{:S(2)}, u32[]{:S(2)}) %collective-permute-start.5) | collective-permute-done | bytes 393248 | tf_op jit(solution)/shard_map/ppermute | solution.py:13
  196.9 2.9 collective-permute-start.6
  199.8 9.4 %collective-permute-done.6 = bf16[1,2,1,2,2,192,1,128]{7,5,4,3,2,1,6,0:T(8,128)(2,1)S(1)} collective-permute-done((bf16[1,2,1,2,2,192,1,128]{7,5,4,3,2,1,6,0:T(8,128)(2,1)S(1)}, bf16[1,2,1,2,2,192,1,128]{7,5,4,3,2,1,6,0:T(8,128)(2,1)S(1)}, u32[]{:S(2)}, u32[]{:S(2)}) %collective-permute-start.6) | collective-permute-done | bytes 393248 | tf_op jit(solution)/shard_map/ppermute | solution.py:13
  211.1 1.9 collective-permute-start.7
  214.3 65.7 %collective-permute-done.7 = bf16[1,1,2,2,2,192,1,128]{7,5,4,3,2,1,6,0:T(8,128)(2,1)S(1)} collective-permute-done((bf16[1,1,2,2,2,192,1,128]{7,5,4,3,2,1,6,0:T(8,128)(2,1)S(1)}, bf16[1,1,2,2,2,192,1,128]{7,5,4,3,2,1,6,0:T(8,128)(2,1)S(1)}, u32[]{:S(2)}, u32[]{:S(2)}) %collective-permute-start.7) | collective-permute-done | bytes 393248 | tf_op jit(solution)/shard_map/ppermute | solution.py:13
  280.8 1.9 multiply_convert_fusion.1
  284.7 34.9 %reduce-scatter.2.cloned.1.call-done = bf16[192,512]{1,0:T(8,128)(2,1)} async-done(((bf16[192,2048]{1,0:T(8,128)(2,1)}), bf16[192,512]{1,0:T(8,128)(2,1)}) %reduce-scatter.2.cloned.1.call-update) | async-done | bytes 196624 | tf_op jit(solution)/shard_map/reduce_scatter | solution.py:135
  319.6 3.2 fusion.23
  322.9 3.1 convolution_add_fusion
  326.0 1.4 add_convert_fusion
  327.4 59.1 %all-reduce.2.cloned.1.call-done = bf16[4,48,3072]{2,1,0:T(8,128)(2,1)} async-done(((bf16[4,48,3072]{2,1,0:T(8,128)(2,1)}), bf16[4,48,3072]{2,1,0:T(8,128)(2,1)}) %all-reduce.2.cloned.1.call-update) | async-done | bytes 1179664 | tf_op jit(solution)/shard_map/psum | solution.py:153
  386.5 1.8 multiply_reduce_fusion.1
  390.5 2.8 fusion.15
  393.3 8.7 %all_gather.3 = bf16[192,2048]{1,0:T(8,128)(2,1)S(1)} all-gather(bf16[192,512]{1,0:T(8,128)(2,1)S(1)} %fusion.15), channel_id=1, replica_groups=mesh['seq'=128,'branch'=4] {'branch'}, dimensions={1}, use_global_device_ids=true | all-gather | bytes 983040 | tf_op jit(solution)/shard_map/all_gather | solution.py:163
  402.0 1.6 fusion.20
  (79 shorter events, 26.2 us)
Async XLA Ops:
  7.9 1.7 copy-start.5
  12.4 1.3 copy-start.4
  17.7 28.0 %collective-permute-start = (bf16[3,2,2,2,1,192,1,128]{7,5,4,3,2,1,6,0:T(8,128)(2,1)}, bf16[3,2,2,2,1,192,1,128]{7,5,4,3,2,1,6,0:T(8,128)(2,1)S(1)}, u32[]{:S(2)}, u32[]{:S(2)}) collective-permute-start(bf16[3,2,2,2,1,192,1,128]{7,5,4,3,2,1,6,0:T(8,128)(2,1)} %constant_dynamic-slice_fusion.7), channel_id=1, source_target_pairs={{0,4},{4,0},{8,12},{12,8},{16,20},{20,16},{24,28},{28,24},{32,36},... | collective-permute-start | bytes 3538952 | tf_op jit(solution)/shard_map/ppermute | solution.py:13
  47.1 31.3 %collective-permute-start.1 = (bf16[3,2,2,1,2,192,1,128]{7,5,4,3,2,1,6,0:T(8,128)(2,1)}, bf16[3,2,2,1,2,192,1,128]{7,5,4,3,2,1,6,0:T(8,128)(2,1)S(1)}, u32[]{:S(2)}, u32[]{:S(2)}) collective-permute-start(bf16[3,2,2,1,2,192,1,128]{7,5,4,3,2,1,6,0:T(8,128)(2,1)} %constant_dynamic-slice_fusion.6), channel_id=1, source_target_pairs={{0,8},{4,12},{8,0},{12,4},{16,24},{20,28},{24,16},{28,20},{32,40},... | collective-permute-start | bytes 3538952 | tf_op jit(solution)/shard_map/ppermute | solution.py:13
  79.7 28.9 %collective-permute-start.2 = (bf16[3,2,1,2,2,192,1,128]{7,5,4,3,2,1,6,0:T(8,128)(2,1)}, bf16[3,2,1,2,2,192,1,128]{7,5,4,3,2,1,6,0:T(8,128)(2,1)S(1)}, u32[]{:S(2)}, u32[]{:S(2)}) collective-permute-start(bf16[3,2,1,2,2,192,1,128]{7,5,4,3,2,1,6,0:T(8,128)(2,1)} %constant_dynamic-slice_fusion.5), channel_id=1, source_target_pairs={{0,16},{4,20},{8,24},{12,28},{16,0},{20,4},{24,8},{28,12},{32,48},... | collective-permute-start | bytes 3538952 | tf_op jit(solution)/shard_map/ppermute | solution.py:13
  84.6 28.8 %copy-start.8 = (bf16[512,24]{0,1:T(8,128)(2,1)S(1)}, bf16[512,24]{0,1:T(8,128)(2,1)}, u32[]{:S(2)}) copy-start(bf16[512,24]{0,1:T(8,128)(2,1)} %param.18) | copy-start | bytes 73732
  109.9 27.3 %collective-permute-start.3 = (bf16[3,1,2,2,2,192,1,128]{7,5,4,3,2,1,6,0:T(8,128)(2,1)}, bf16[3,1,2,2,2,192,1,128]{7,5,4,3,2,1,6,0:T(8,128)(2,1)S(1)}, u32[]{:S(2)}, u32[]{:S(2)}) collective-permute-start(bf16[3,1,2,2,2,192,1,128]{7,5,4,3,2,1,6,0:T(8,128)(2,1)} %constant_dynamic-slice_fusion.4), channel_id=1, source_target_pairs={{0,32},{4,36},{8,40},{12,44},{16,48},{20,52},{24,56},{28,60},{32,0... | collective-permute-start | bytes 3538952 | tf_op jit(solution)/shard_map/ppermute | solution.py:13
  115.3 204.4 %all-to-all-start = ((bf16[128,512,24]{1,2,0:T(8,128)(2,1)}), bf16[128,512,24]{1,2,0:T(8,128)(2,1)}, u32[]{:S(2)}, u32[]{:S(2)}) async-start(bf16[128,512,24]{1,2,0:T(8,128)(2,1)} %stack.14), calls=%async_computation.1 | async-start | bytes 6291456 | tf_op jit(solution)/shard_map/all_to_all | solution.py:133
  136.9 182.7 %reduce-scatter.2.cloned.1.call-start = ((), (), s32[]{:S(2)}) async-start(), calls=%async_computation.2 | async-start | bytes 983040 | tf_op jit(solution)/shard_map/reduce_scatter | solution.py:135
  140.7 1.2 copy-start.2
  145.9 1.2 copy-start.2
  151.1 1.2 copy-start.2
  156.3 1.2 copy-start.2
  161.5 1.2 copy-start.2
  166.7 1.2 copy-start.2
  171.0 42.7 %copy-start.9 = (f32[64]{0:T(128)S(1)}, f32[64]{0:T(128)}, u32[]{:S(2)}) copy-start(f32[64]{0:T(128)} %param.17) | copy-start | bytes 772
  171.0 11.8 %collective-permute-start.4 = (bf16[1,2,2,2,1,192,1,128]{7,5,4,3,2,1,6,0:T(8,128)(2,1)S(1)}, bf16[1,2,2,2,1,192,1,128]{7,5,4,3,2,1,6,0:T(8,128)(2,1)S(1)}, u32[]{:S(2)}, u32[]{:S(2)}) collective-permute-start(bf16[1,2,2,2,1,192,1,128]{7,5,4,3,2,1,6,0:T(8,128)(2,1)S(1)} %constant_dynamic-slice_fusion.3), channel_id=1, source_target_pairs={{0,4},{4,0},{8,12},{12,8},{16,20},{20,16},{24,28},{28,24},{32,36},... | collective-permute-start | bytes 1179656 | tf_op jit(solution)/shard_map/ppermute | solution.py:13
  184.6 10.4 %collective-permute-start.5 = (bf16[1,2,2,1,2,192,1,128]{7,5,4,3,2,1,6,0:T(8,128)(2,1)S(1)}, bf16[1,2,2,1,2,192,1,128]{7,5,4,3,2,1,6,0:T(8,128)(2,1)S(1)}, u32[]{:S(2)}, u32[]{:S(2)}) collective-permute-start(bf16[1,2,2,1,2,192,1,128]{7,5,4,3,2,1,6,0:T(8,128)(2,1)S(1)} %constant_dynamic-slice_fusion.2), channel_id=1, source_target_pairs={{0,8},{4,12},{8,0},{12,4},{16,24},{20,28},{24,16},{28,20},{32,40},... | collective-permute-start | bytes 1179656 | tf_op jit(solution)/shard_map/ppermute | solution.py:13
  196.9 12.3 %collective-permute-start.6 = (bf16[1,2,1,2,2,192,1,128]{7,5,4,3,2,1,6,0:T(8,128)(2,1)S(1)}, bf16[1,2,1,2,2,192,1,128]{7,5,4,3,2,1,6,0:T(8,128)(2,1)S(1)}, u32[]{:S(2)}, u32[]{:S(2)}) collective-permute-start(bf16[1,2,1,2,2,192,1,128]{7,5,4,3,2,1,6,0:T(8,128)(2,1)S(1)} %constant_dynamic-slice_fusion.1), channel_id=1, source_target_pairs={{0,16},{4,20},{8,24},{12,28},{16,0},{20,4},{24,8},{28,12},{32,48},... | collective-permute-start | bytes 1179656 | tf_op jit(solution)/shard_map/ppermute | solution.py:13
  211.1 68.9 %collective-permute-start.7 = (bf16[1,1,2,2,2,192,1,128]{7,5,4,3,2,1,6,0:T(8,128)(2,1)S(1)}, bf16[1,1,2,2,2,192,1,128]{7,5,4,3,2,1,6,0:T(8,128)(2,1)S(1)}, u32[]{:S(2)}, u32[]{:S(2)}) collective-permute-start(bf16[1,1,2,2,2,192,1,128]{7,5,4,3,2,1,6,0:T(8,128)(2,1)S(1)} %constant_dynamic-slice_fusion), channel_id=1, source_target_pairs={{0,32},{4,36},{8,40},{12,44},{16,48},{20,52},{24,56},{28,60},{32,0... | collective-permute-start | bytes 1179656 | tf_op jit(solution)/shard_map/ppermute | solution.py:13
  282.7 2.0 copy-start.6
  284.6 101.8 %all-reduce.2.cloned.1.call-start = ((), (), s32[]{:S(2)}) async-start(), calls=%async_computation.3 | async-start | bytes 2359296 | tf_op jit(solution)/shard_map/psum | solution.py:153
  319.6 3.2 copy-start.3
  326.0 60.5 %copy-start.1 = (bf16[192,3072]{1,0:T(8,128)(2,1)S(1)}, bf16[192,3072]{1,0:T(8,128)(2,1)}, u32[]{:S(2)}) copy-start(bf16[192,3072]{1,0:T(8,128)(2,1)} %param.21) | copy-start | bytes 3538948
  326.0 60.5 %copy-start.7 = (f32[3072]{0:T(1024)S(1)}, f32[3072]{0:T(1024)}, u32[]{:S(2)}) copy-start(f32[3072]{0:T(1024)} %param.20) | copy-start | bytes 36868
  386.5 2.4 copy-start
Sparse Core Ops, SparseCore 0:
  284.7 34.8 reduce-scatter.1
  327.5 58.8 all-reduce.1
